TPU v7x, 512 devices: a whole 4x8x8 slice. The times are simulated.
512 devices in a mesh: fib: 64 (over z, x, core), pln: 8 (over y).
Axes of the slice: x: 4, y: 8, z: 8, core: 2. Of those that a mesh axis runs over, the one named last changes fastest.
Arguments:
- nodal_values: float32 [8, 64, 288, 1000], P('pln', 'fib'), may hold values from -6 to 6
- interp_matrix: float32 [1000, 512], replicated, may hold values from -0.1875 to 0.1875
- count_table: int32 [8, 64, 3], P('pln'), may hold values from 1 to 96, as said below
- slot_order: int32 [8, 64, 192], P('pln', 'fib'), may hold values from 0 to 191, each once within a row
- start_basis: float32 [768, 128], replicated, may hold values from -6 to 6
Outputs:
- core_values: float32 [8, 64, 128, 128], P('pln', 'fib')
Inputs may be any that keep to these rules, and one draw needn't show every extreme that they name: count_table[j, o, d] elements of owner o come from the source d places before it along fib, cyclically; for every owner the 3 entries sum to 192 and one equals 96. `slot_order`: each owner's row is a permutation.
All inputs are finite; a program needn't handle non-finite values.
Results may differ from a plain program's by a relative error of at most 0.0003.
Values sent between devices are 32-bit elements; how exact they have to be, the bound alone decides.
A program may use at most 64 MiB of HBM per device.

v0:
```python
import jax
import jax.numpy as jnp
from jax import lax
from jax.sharding import PartitionSpec as P

NX = 768
TILES_DEV = 1


def shifted(value, axis, by):
    peers = lax.axis_size(axis)
    return lax.ppermute(value, axis, [(i, (i + by) % peers) for i in range(peers)])


def per_device(nodal_values, interp_matrix, count_table, slot_order, start_basis):
    full_precision = lax.Precision.HIGHEST
    node_rows = nodal_values[0, 0]
    owner_table = count_table[0]
    brick_order = slot_order[0, 0]
    owners = lax.axis_size("fib")
    own_index = lax.axis_index("fib")
    window = owner_table.shape[1]
    capacity = node_rows.shape[0] // window
    elements = brick_order.shape[0]
    tiles_total = TILES_DEV * owners
    block_width = NX // owners
    send_start = []
    running = jnp.int32(0)
    for distance in range(window):
        send_start.append(running)
        column = owner_table[:, distance]
        running = running + lax.dynamic_index_in_dim(
            column, (own_index + distance) % owners, 0, keepdims=False
        )
    own_counts = lax.dynamic_index_in_dim(owner_table, own_index, 0, keepdims=False)
    positions = jnp.arange(elements, dtype=jnp.int32)
    combined_index = jnp.zeros((elements,), jnp.int32)
    offset = jnp.int32(0)
    for distance in range(window - 1, -1, -1):
        taken_count = own_counts[distance]
        inside = (positions >= offset) & (positions < offset + taken_count)
        combined_index = jnp.where(inside, distance * capacity + positions - offset, combined_index)
        offset = offset + taken_count
    brick_source = jnp.zeros((elements,), jnp.int32).at[brick_order].set(combined_index)
    grid_rows = jnp.dot(
        node_rows, interp_matrix, precision=full_precision, preferred_element_type=jnp.float32
    )
    received = []
    for distance in range(window):
        send_piece = lax.dynamic_slice_in_dim(grid_rows, send_start[distance], capacity, 0)
        if distance > 0:
            send_piece = shifted(send_piece, "fib", distance)
        received.append(send_piece)
    brick_values = jnp.concatenate(received, axis=0)[brick_source]
    brick_grid = brick_values.reshape(tiles_total, block_width, brick_values.shape[1] // 4)
    fibre_field = lax.all_to_all(brick_grid, "fib", split_axis=0, concat_axis=1, tiled=True)
    gram_part = jnp.einsum("txf,tyf->xy", fibre_field, fibre_field, precision=full_precision)
    gram_matrix = lax.psum(gram_part, ("fib", "pln"))
    image_matrix = jnp.dot(gram_matrix, start_basis, precision=full_precision)
    normal_matrix = jnp.dot(image_matrix.T, image_matrix, precision=full_precision)
    lower_factor = jnp.linalg.cholesky(normal_matrix)
    new_basis = jax.scipy.linalg.solve_triangular(lower_factor, image_matrix.T, lower=True).T
    core_values = jnp.einsum("xk,txf->tkf", new_basis, fibre_field, precision=full_precision)
    return core_values[None]


def solution(mesh):
    placed = (P("pln", "fib", None, None), P(), P("pln", None, None), P("pln", "fib", None), P())
    return jax.shard_map(
        per_device,
        mesh=mesh,
        in_specs=placed,
        out_specs=P("pln", "fib", None, None),
        check_vma=False,
    )
```

profile of v0, /device:TPU:1, one launch (start us, length us, event | category | flops | bytes accessed | tf_op | source)
XLA Modules:
  0.0 377.5 jit_solution(10091446328949841219)
XLA Ops:
  6.5 0.0 copy-start
  6.5 0.0 all-reduce.2.cloned.1.call-start
  6.5 0.8 copy.12
  7.4 0.7 constant_dynamic-slice_fusion.4
  11.2 0.0 copy-done
  11.2 0.0 copy-start.2
  11.2 0.0 copy-start.3
  11.2 3.4 fusion
  14.7 0.1 fusion.8
  14.7 3.9 %collective-permute-start.1 = (f32[96,512]{1,0:T(8,128)S(1)}, f32[96,512]{1,0:T(8,128)S(1)}, u32[]{:S(2)}, u32[]{:S(2)}) collective-permute-start(f32[96,512]{1,0:T(8,128)S(1)} %get-tuple-element.6), channel_id=1, source_target_pairs={{0,16},{8,24},{16,32},{24,40},{32,48},{40,56},{48,64},{56,72},{64,... | collective-permute-start | bytes 589832 | tf_op jit(solution)/shard_map/ppermute | solution.py:12
  18.7 4.0 %collective-permute-start = (f32[96,512]{1,0:T(8,128)S(1)}, f32[96,512]{1,0:T(8,128)S(1)}, u32[]{:S(2)}, u32[]{:S(2)}) collective-permute-start(f32[96,512]{1,0:T(8,128)S(1)} %get-tuple-element.7), channel_id=1, source_target_pairs={{0,8},{8,16},{16,24},{24,32},{32,40},{40,48},{48,56},{56,64},{64,7... | collective-permute-start | bytes 589832 | tf_op jit(solution)/shard_map/ppermute | solution.py:12
  22.6 0.0 copy-done.2
  22.6 0.7 constant_dynamic-slice_fusion.2
  25.2 0.6 and_select_fusion.1
  25.8 0.0 copy-done.3
  25.8 1.2 scatter_custom_fusion
  27.1 5.9 %collective-permute-done.1 = f32[96,512]{1,0:T(8,128)S(1)} collective-permute-done((f32[96,512]{1,0:T(8,128)S(1)}, f32[96,512]{1,0:T(8,128)S(1)}, u32[]{:S(2)}, u32[]{:S(2)}) %collective-permute-start.1) | collective-permute-done | bytes 196640 | tf_op jit(solution)/shard_map/ppermute | solution.py:12
  33.0 0.0 collective-permute-done
  33.0 0.9 gather_fusion
  33.9 0.1 reshape.65
  34.0 25.5 %all_to_all.4 = f32[64,12,128]{2,1,0:T(8,128)S(1)} all-to-all(f32[64,12,128]{2,1,0:T(8,128)S(1)} %reshape.65), channel_id=1, replica_groups=mesh['fib'=64,'pln'=8] {'fib'}, dimensions={0} | all-to-all | bytes 786432 | tf_op jit(solution)/shard_map/all_to_all | solution.py:56
  59.6 0.0 copy-start.1
  59.6 3.4 fusion.10
  63.0 0.0 all-reduce.2.cloned.1.call-update
  63.0 278.1 %all-reduce.2.cloned.1.call-done = f32[768,768]{1,0:T(8,128)} async-done(((f32[768,768]{1,0:T(8,128)}), f32[768,768]{1,0:T(8,128)}) %all-reduce.2.cloned.1.call-update) | async-done | bytes 2359312 | tf_op jit(solution)/shard_map/psum | solution.py:58
  341.1 0.0 copy-done.1
  341.1 3.7 fusion.11
  344.8 0.8 fusion.12
  345.6 0.1 copy.8
  345.7 11.7 %cholesky.16 = f32[128,128]{1,0:T(8,128)S(1)} custom-call(f32[128,128]{1,0:T(8,128)S(1)} %fusion.5), custom_call_target="Cholesky" | custom-call | tf_op jit(solution)/shard_map/jit(cholesky)/cholesky | solution.py:61
  357.4 0.6 compare_reduce_fusion
  358.1 0.7 fusion.2
  358.8 9.8 %custom-call.7 = f32[1,128,128]{1,2,0:T(8,128)S(1)} custom-call(f32[1,128,128]{2,1,0:T(8,128)S(1)} %fusion.2), custom_call_target="InvertDiagBlocksLowerTriangular" | custom-call | tf_op jit(solution)/shard_map/jit(_solve_triangular)/triangular_solve | solution.py:62
  368.6 0.5 fusion.3
  369.1 0.8 convolution_bitcast_fusion
  369.9 0.7 copy.9
  (8 shorter events, 0.1 us)
Async XLA Ops:
  6.5 4.7 %copy-start = (f32[1000,512]{1,0:T(8,128)S(1)}, f32[1000,512]{1,0:T(8,128)}, u32[]{:S(2)}) copy-start(f32[1000,512]{1,0:T(8,128)} %param.6) | copy-start | bytes 6144004
  6.5 334.6 %all-reduce.2.cloned.1.call-start = ((), (), s32[]{:S(2)}) async-start(), calls=%async_computation.1 | async-start | bytes 4718592 | tf_op jit(solution)/shard_map/psum | solution.py:58
  11.2 11.4 %copy-start.2 = (s32[1,64,3]{1,0,2:T(1,128)S(1)}, s32[1,64,3]{1,0,2:T(1,128)}, u32[]{:S(2)}) copy-start(s32[1,64,3]{1,0,2:T(1,128)} %param.7) | copy-start | bytes 2308
  11.2 14.6 %copy-start.3 = (s32[1,1,192]{2,1,0:T(1,128)S(1)}, s32[1,1,192]{2,1,0:T(1,128)}, u32[]{:S(2)}) copy-start(s32[1,1,192]{2,1,0:T(1,128)} %param.8) | copy-start | bytes 2308
  14.7 18.3 %collective-permute-start.1 = (f32[96,512]{1,0:T(8,128)S(1)}, f32[96,512]{1,0:T(8,128)S(1)}, u32[]{:S(2)}, u32[]{:S(2)}) collective-permute-start(f32[96,512]{1,0:T(8,128)S(1)} %get-tuple-element.6), channel_id=1, source_target_pairs={{0,16},{8,24},{16,32},{24,40},{32,48},{40,56},{48,64},{56,72},{64,... | collective-permute-start | bytes 589832 | tf_op jit(solution)/shard_map/ppermute | solution.py:12
  18.7 14.3 %collective-permute-start = (f32[96,512]{1,0:T(8,128)S(1)}, f32[96,512]{1,0:T(8,128)S(1)}, u32[]{:S(2)}, u32[]{:S(2)}) collective-permute-start(f32[96,512]{1,0:T(8,128)S(1)} %get-tuple-element.7), channel_id=1, source_target_pairs={{0,8},{8,16},{16,24},{24,32},{32,40},{40,48},{48,56},{56,64},{64,7... | collective-permute-start | bytes 589832 | tf_op jit(solution)/shard_map/ppermute | solution.py:12
  59.6 281.6 %copy-start.1 = (f32[768,128]{1,0:T(8,128)S(1)}, f32[768,128]{1,0:T(8,128)}, u32[]{:S(2)}) copy-start(f32[768,128]{1,0:T(8,128)} %param.9) | copy-start | bytes 1179652
Sparse Core Ops, SparseCore 0:
  63.1 277.9 all-reduce.1
where the time goes:
time: 378 us; the launch traced here: 377 us
  waiting for transfers between devices  284 us (75%)
  blocking collectives  25.5 us (7%)
  other arithmetic  23.5 us (6%)
  between operations  18.7 us (5%)
  matrix products  12.6 us (3%)
  starting transfers between devices  7.9 us (2%)
  local copies, waits for them, and re-layouts  5.23 us (1%)
    psum x1, waiting for transfers between devices, per_device(): gram_matrix = lax.psum(gram_part, ('fib', 'pln'))  278 us
    all_to_all x1, blocking collectives, per_device(): lax.all_to_all(brick_grid, 'fib', split_axis=0, concat_axis=1, tiled=True)  25.5 us
    another operation x3, other arithmetic, per_device(): lower_factor = jnp.linalg.cholesky(normal_matrix)  12.4 us
    another operation x2, other arithmetic, per_device(): jax.scipy.linalg.solve_triangular(lower_factor, image_matrix.T, lower=True)  10.5 us
    ppermute x2, starting transfers between devices, shifted(): lax.ppermute(value, axis, [(i, (i + by) % peers) for i in range(peers)])  7.89 us
  transfers between devices with their start and end apart: 3, of which 2 were waited for; matrix products, arithmetic and copies ran while one was open for 1% of the time, Pallas kernels for 0%

commit v1 on v0

--- a/solution.py
+++ b/solution.py
@@ -55,7 +55,7 @@
     brick_grid = brick_values.reshape(tiles_total, block_width, brick_values.shape[1] // 4)
     fibre_field = lax.all_to_all(brick_grid, "fib", split_axis=0, concat_axis=1, tiled=True)
     gram_part = jnp.einsum("txf,tyf->xy", fibre_field, fibre_field, precision=full_precision)
-    gram_matrix = lax.psum(gram_part, ("fib", "pln"))
+    gram_matrix = lax.psum(lax.psum(gram_part, "fib"), "pln")
     image_matrix = jnp.dot(gram_matrix, start_basis, precision=full_precision)
     normal_matrix = jnp.dot(image_matrix.T, image_matrix, precision=full_precision)
     lower_factor = jnp.linalg.cholesky(normal_matrix)

time: 378 us -> 387 us (1.024)
  waiting for transfers between devices: 284 us -> 291 us
    psum x1 -> x2, waiting for transfers between devices: 278 us -> 285 us  [per_device(): gram_matrix = lax.psum(lax.psum(gram_part, 'fib'), 'pln')]
  transfers between devices with their start and end apart: 3 -> 4, of which waited for: 2 -> 3; matrix products, arithmetic and copies ran while one was open for 1% -> 1% of each run, Pallas kernels for 0% -> 0%
where the time goes in v1:
time: 387 us; the launch traced here: 384 us
  waiting for transfers between devices  291 us (75%)
  blocking collectives  25.5 us (7%)
  other arithmetic  23.5 us (6%)
  between operations  18.7 us (5%)
  matrix products  12.6 us (3%)
  starting transfers between devices  8.12 us (2%)
  local copies, waits for them, and re-layouts  5.23 us (1%)
    psum x2, waiting for transfers between devices, per_device(): gram_matrix = lax.psum(lax.psum(gram_part, 'fib'), 'pln')  285 us
    all_to_all x1, blocking collectives, per_device(): lax.all_to_all(brick_grid, 'fib', split_axis=0, concat_axis=1, tiled=True)  25.5 us
    another operation x3, other arithmetic, per_device(): lower_factor = jnp.linalg.cholesky(normal_matrix)  12.4 us
    another operation x2, other arithmetic, per_device(): jax.scipy.linalg.solve_triangular(lower_factor, image_matrix.T, lower=True)  10.5 us
    ppermute x2, starting transfers between devices, shifted(): lax.ppermute(value, axis, [(i, (i + by) % peers) for i in range(peers)])  7.89 us
  transfers between devices with their start and end apart: 4, of which 3 were waited for; matrix products, arithmetic and copies ran while one was open for 1% of the time, Pallas kernels for 0%

profile of v1, /device:TPU:1, one launch (start us, length us, event | category | flops | bytes accessed | tf_op | source)
XLA Modules:
  0.0 384.3 jit_solution(14774030590271459519)
XLA Ops:
  6.5 0.0 copy-start
  6.5 0.0 all-reduce.3.cloned.1.call-start
  6.5 0.8 copy.12
  7.4 0.7 constant_dynamic-slice_fusion.4
  11.2 0.0 copy-done
  11.2 0.0 copy-start.2
  11.2 0.0 copy-start.3
  11.2 3.4 fusion
  14.7 0.1 fusion.8
  14.7 3.9 %collective-permute-start.1 = (f32[96,512]{1,0:T(8,128)S(1)}, f32[96,512]{1,0:T(8,128)S(1)}, u32[]{:S(2)}, u32[]{:S(2)}) collective-permute-start(f32[96,512]{1,0:T(8,128)S(1)} %get-tuple-element.6), channel_id=1, source_target_pairs={{0,16},{8,24},{16,32},{24,40},{32,48},{40,56},{48,64},{56,72},{64,... | collective-permute-start | bytes 589832 | tf_op jit(solution)/shard_map/ppermute | solution.py:12
  18.7 4.0 %collective-permute-start = (f32[96,512]{1,0:T(8,128)S(1)}, f32[96,512]{1,0:T(8,128)S(1)}, u32[]{:S(2)}, u32[]{:S(2)}) collective-permute-start(f32[96,512]{1,0:T(8,128)S(1)} %get-tuple-element.7), channel_id=1, source_target_pairs={{0,8},{8,16},{16,24},{24,32},{32,40},{40,48},{48,56},{56,64},{64,7... | collective-permute-start | bytes 589832 | tf_op jit(solution)/shard_map/ppermute | solution.py:12
  22.6 0.0 copy-done.2
  22.6 0.7 constant_dynamic-slice_fusion.2
  25.2 0.6 and_select_fusion.1
  25.8 0.0 copy-done.3
  25.8 1.2 scatter_custom_fusion
  27.1 5.9 %collective-permute-done.1 = f32[96,512]{1,0:T(8,128)S(1)} collective-permute-done((f32[96,512]{1,0:T(8,128)S(1)}, f32[96,512]{1,0:T(8,128)S(1)}, u32[]{:S(2)}, u32[]{:S(2)}) %collective-permute-start.1) | collective-permute-done | bytes 196640 | tf_op jit(solution)/shard_map/ppermute | solution.py:12
  33.0 0.0 collective-permute-done
  33.0 0.9 gather_fusion
  33.9 0.1 reshape.65
  34.0 25.5 %all_to_all.4 = f32[64,12,128]{2,1,0:T(8,128)S(1)} all-to-all(f32[64,12,128]{2,1,0:T(8,128)S(1)} %reshape.65), channel_id=1, replica_groups=mesh['fib'=64,'pln'=8] {'fib'}, dimensions={0} | all-to-all | bytes 786432 | tf_op jit(solution)/shard_map/all_to_all | solution.py:56
  59.6 3.4 fusion.10
  63.0 0.0 copy-start.1
  63.0 0.0 all-reduce.3.cloned.1.call-update
  63.0 0.2 all-reduce.5.cloned.1.call-start
  63.2 197.0 %all-reduce.3.cloned.1.call-done = f32[768,768]{1,0:T(8,128)} async-done(((f32[768,768]{1,0:T(8,128)}), f32[768,768]{1,0:T(8,128)}) %all-reduce.3.cloned.1.call-update) | async-done | bytes 2359312 | tf_op jit(solution)/shard_map/psum | solution.py:58
  260.3 0.0 all-reduce.5.cloned.1.call-update
  260.3 87.6 %all-reduce.5.cloned.1.call-done = f32[768,768]{1,0:T(8,128)} async-done(((f32[768,768]{1,0:T(8,128)}), f32[768,768]{1,0:T(8,128)}) %all-reduce.5.cloned.1.call-update) | async-done | bytes 2359312 | tf_op jit(solution)/shard_map/psum | solution.py:58
  347.9 0.0 copy-done.1
  347.9 3.7 fusion.11
  351.6 0.8 fusion.12
  352.4 0.1 copy.8
  352.5 11.7 %cholesky.16 = f32[128,128]{1,0:T(8,128)S(1)} custom-call(f32[128,128]{1,0:T(8,128)S(1)} %fusion.5), custom_call_target="Cholesky" | custom-call | tf_op jit(solution)/shard_map/jit(cholesky)/cholesky | solution.py:61
  364.2 0.6 compare_reduce_fusion
  364.9 0.7 fusion.2
  365.5 9.8 %custom-call.7 = f32[1,128,128]{1,2,0:T(8,128)S(1)} custom-call(f32[1,128,128]{2,1,0:T(8,128)S(1)} %fusion.2), custom_call_target="InvertDiagBlocksLowerTriangular" | custom-call | tf_op jit(solution)/shard_map/jit(_solve_triangular)/triangular_solve | solution.py:62
  375.4 0.5 fusion.3
  375.9 0.8 convolution_bitcast_fusion
  376.7 0.7 copy.9
  (8 shorter events, 0.1 us)
Async XLA Ops:
  6.5 4.7 %copy-start = (f32[1000,512]{1,0:T(8,128)S(1)}, f32[1000,512]{1,0:T(8,128)}, u32[]{:S(2)}) copy-start(f32[1000,512]{1,0:T(8,128)} %param.6) | copy-start | bytes 6144004
  6.5 253.7 %all-reduce.3.cloned.1.call-start = ((), (), s32[]{:S(2)}) async-start(), calls=%async_computation.1 | async-start | bytes 4718592 | tf_op jit(solution)/shard_map/psum | solution.py:58
  11.2 11.4 %copy-start.2 = (s32[1,64,3]{1,0,2:T(1,128)S(1)}, s32[1,64,3]{1,0,2:T(1,128)}, u32[]{:S(2)}) copy-start(s32[1,64,3]{1,0,2:T(1,128)} %param.7) | copy-start | bytes 2308
  11.2 14.6 %copy-start.3 = (s32[1,1,192]{2,1,0:T(1,128)S(1)}, s32[1,1,192]{2,1,0:T(1,128)}, u32[]{:S(2)}) copy-start(s32[1,1,192]{2,1,0:T(1,128)} %param.8) | copy-start | bytes 2308
  14.7 18.3 %collective-permute-start.1 = (f32[96,512]{1,0:T(8,128)S(1)}, f32[96,512]{1,0:T(8,128)S(1)}, u32[]{:S(2)}, u32[]{:S(2)}) collective-permute-start(f32[96,512]{1,0:T(8,128)S(1)} %get-tuple-element.6), channel_id=1, source_target_pairs={{0,16},{8,24},{16,32},{24,40},{32,48},{40,56},{48,64},{56,72},{64,... | collective-permute-start | bytes 589832 | tf_op jit(solution)/shard_map/ppermute | solution.py:12
  18.7 14.3 %collective-permute-start = (f32[96,512]{1,0:T(8,128)S(1)}, f32[96,512]{1,0:T(8,128)S(1)}, u32[]{:S(2)}, u32[]{:S(2)}) collective-permute-start(f32[96,512]{1,0:T(8,128)S(1)} %get-tuple-element.7), channel_id=1, source_target_pairs={{0,8},{8,16},{16,24},{24,32},{32,40},{40,48},{48,56},{56,64},{64,7... | collective-permute-start | bytes 589832 | tf_op jit(solution)/shard_map/ppermute | solution.py:12
  63.0 284.9 %copy-start.1 = (f32[768,128]{1,0:T(8,128)S(1)}, f32[768,128]{1,0:T(8,128)}, u32[]{:S(2)}) copy-start(f32[768,128]{1,0:T(8,128)} %param.9) | copy-start | bytes 1179652
  63.0 284.9 %all-reduce.5.cloned.1.call-start = ((), (), s32[]{:S(2)}) async-start(), calls=%async_computation.2 | async-start | bytes 4718592 | tf_op jit(solution)/shard_map/psum | solution.py:58
Sparse Core Ops, SparseCore 0:
  63.1 197.0 all-reduce.2
  262.6 85.2 all-reduce.4
